TPU v7x, 256 devices: a whole 4x4x8 slice. The times are simulated.
256 devices in a mesh: section: 2 (over z_lo), seq: 32 (over x, z_hi, core), tp: 4 (over y).
Axes of the slice: x: 4, y: 4, z: 8 (z_hi: 4, z_lo: 2; z = z_hi * 2 + z_lo), core: 2. Of those that a mesh axis runs over, the one named last changes fastest.
Arguments:
- hidden: bfloat16 [1024, 3072], P('seq', 'tp'), may hold values from -6 to 6
- qkv_weight: bfloat16 [2, 3072, 3, 1536], P('section', None, None, 'tp'), may hold values from -0.109375 to 0.109375
- qk_gain: float32 [2, 2, 64], P('section'), may hold values from 1.3 to 2
- out_weight: bfloat16 [2, 1536, 3072], P('section', 'tp'), may hold values from -0.15625 to 0.15625
- mod_weight: bfloat16 [2, 512, 18432], P('section', None, ('seq', 'tp')), may hold values from -0.5 to 0.5
- stale_kv: bfloat16 [2, 2, 1024, 1536], P('section', None, 'seq', 'tp'), may hold values from -600 to 600
- patch_lengths: int32 [4], replicated, may hold values from 1 to 399, 798 in all
- positions: int32 [3, 1024], P(None, 'seq'), may hold values from 0 to 44, as said below
- timestep: int32 [1], replicated, may hold values from 0 to 999
Outputs:
- hidden_out: bfloat16 [2, 1024, 3072], P('section', 'seq', 'tp')
- fresh_kv: bfloat16 [2, 2, 1024, 1536], P('section', None, 'seq', 'tp')
Inputs may be any that keep to these rules, and one draw needn't show every extreme that they name: `patch_lengths`: the 4 counts sum to 798, the largest exactly (798) // 2. `positions`: frames lie below 13, rows below 30, columns below 45.
All inputs are finite; a program needn't handle non-finite values.
Results may differ from a plain program's by a relative error of at most 0.025.
Values may be sent and summed in bfloat16 or wider, within the bound.
A program may use at most 64 MiB of HBM per device.

v0:
```python
import math
import jax
import jax.numpy as jnp
from jax import lax
from jax.sharding import PartitionSpec as P

HEAD = 64
TEMB = 512
TEXT = 226


def shifted(value, axis, steps):
    count = lax.axis_size(axis)
    first, last = (max(0, -steps), min(count, count - steps))
    return lax.ppermute(value, axis, [(source, source + steps) for source in range(first, last)])


def patch_index(index, bounds):
    video_row = index - TEXT
    patch_id = jnp.sum((video_row[:, None] >= bounds[None, :-1]).astype(jnp.int32), axis=1)
    return jnp.where(index < TEXT, 0, patch_id)


def time_features(timestep):
    half_width = TEMB // 2
    frequency = jnp.exp(
        -math.log(10000.0) * jnp.arange(half_width).astype(jnp.float32) / half_width
    )
    phases = timestep.astype(jnp.float32)[:, None] * frequency[None, :]
    embedded = jnp.concatenate([jnp.cos(phases), jnp.sin(phases)], axis=1)
    return jax.nn.silu(embedded).astype(jnp.bfloat16)


def axis_freq(dim_size):
    return 1.0 / 10000.0 ** (jnp.arange(0, dim_size, 2).astype(jnp.float32) / dim_size)


def rope_tables(positions, head_count):
    coords = positions.astype(jnp.float32)
    angles = jnp.concatenate(
        [
            coords[0][:, None] * axis_freq(HEAD // 4)[None, :],
            coords[1][:, None] * axis_freq(3 * HEAD // 8)[None, :],
            coords[2][:, None] * axis_freq(3 * HEAD // 8)[None, :],
        ],
        axis=1,
    )
    angles = jnp.repeat(angles, 2, axis=1)
    return (jnp.tile(jnp.cos(angles), (1, head_count)), jnp.tile(jnp.sin(angles), (1, head_count)))


def rotate_pairs(values):
    column = jnp.arange(values.shape[-1])
    return jnp.where(column % 2 == 0, -jnp.roll(values, -1, axis=-1), jnp.roll(values, 1, axis=-1))


def head_norm(values, gain):
    parts = values.reshape(values.shape[0], -1, HEAD)
    average = jnp.mean(parts, axis=-1, keepdims=True)
    centred = parts - average
    variance = jnp.mean(centred * centred, axis=-1, keepdims=True)
    return (centred * lax.rsqrt(variance + 1e-06) * gain).reshape(values.shape)


def merge_block(running, query_heads, query_patch, fresh_block, stale_block, bounds):
    highest, denominator, accumulated = running
    key_count = fresh_block.shape[1]
    head_count = query_heads.shape[1]
    key_rows = jnp.arange(key_count, dtype=jnp.int32)
    allowed = (patch_index(key_rows, bounds)[None, :] <= query_patch[:, None])[None]
    fresh_keys = fresh_block[0].reshape(key_count, head_count, HEAD)
    fresh_vals = fresh_block[1].reshape(key_count, head_count, HEAD)
    stale_keys = stale_block[0].reshape(key_count, head_count, HEAD)
    stale_vals = stale_block[1].reshape(key_count, head_count, HEAD)
    scores_fresh = jnp.einsum(
        "thd,rhd->htr", query_heads, fresh_keys, preferred_element_type=jnp.float32
    )
    scores_stale = jnp.einsum(
        "thd,rhd->htr", query_heads, stale_keys, preferred_element_type=jnp.float32
    )
    scores = jnp.where(allowed, scores_fresh, scores_stale) * HEAD ** (-0.5)
    new_high = jnp.maximum(highest, jnp.max(scores, axis=2))
    rescale = jnp.exp(highest - new_high)
    weights_soft = jnp.exp(scores - new_high[:, :, None])
    denominator = jnp.sum(weights_soft, axis=2)
    part_fresh = jnp.where(allowed, weights_soft, 0.0).astype(jnp.bfloat16)
    part_stale = jnp.where(allowed, 0.0, weights_soft).astype(jnp.bfloat16)
    accumulated = accumulated * rescale[:, :, None]
    accumulated = jnp.einsum(
        "htr,rhd->htd", part_fresh, fresh_vals, preferred_element_type=jnp.float32
    )
    accumulated = accumulated + jnp.einsum(
        "htr,rhd->htd", part_stale, stale_vals, preferred_element_type=jnp.float32
    )
    return (new_high, denominator, accumulated)


def local(
    hidden,
    qkv_weight,
    qk_gain,
    out_weight,
    mod_weight,
    stale_kv,
    patch_lengths,
    positions,
    timestep,
):
    tok_rows = hidden.shape[0]
    feat_share = hidden.shape[1]
    model_width = feat_share * lax.axis_size("tp")
    head_cols = qkv_weight.shape[3]
    head_count = head_cols // HEAD
    seq_rank = lax.axis_index("seq")
    tp_rank = lax.axis_index("tp")
    section_rank = lax.axis_index("section")
    mod_share = jnp.dot(time_features(timestep), mod_weight[0], preferred_element_type=jnp.float32)[
        0
    ]
    by_tp = lax.all_gather(mod_share[None, None, :], "tp", axis=0, tiled=True)
    modulate = lax.all_gather(
        jnp.pad(by_tp.reshape(1, 4, -1), ((0, 0), (0, 4), (0, 0))), "seq", axis=0, tiled=True
    )[:, :4].reshape(6, model_width)
    my_rows = seq_rank * tok_rows + jnp.arange(tok_rows, dtype=jnp.int32)
    video = (my_rows >= TEXT)[:, None]
    bounds = jnp.cumsum(patch_lengths)
    query_patch = patch_index(my_rows, bounds)
    cosine, sine_table = rope_tables(positions, head_count)
    shift_rows = jnp.where(video, modulate[0], modulate[3])
    scale_rows = jnp.where(video, modulate[1], modulate[4])
    gate_both = lax.dynamic_slice_in_dim(modulate, tp_rank * feat_share, feat_share, 1)
    gate_rows = jnp.where(video, gate_both[2], gate_both[5])
    weights_qkv = qkv_weight[0]
    gains = qk_gain[0]
    weights_out = out_weight[0]
    stale_own = stale_kv[0]

    def attend(queries, fresh_kv):
        query_heads = queries.reshape(tok_rows, head_count, HEAD)
        start_state = (
            jnp.full((head_count, tok_rows), -1e30, jnp.float32),
            jnp.zeros((head_count, tok_rows), jnp.float32),
            jnp.zeros((head_count, tok_rows, HEAD), jnp.float32),
        )
        highest, denominator, accumulated = merge_block(
            start_state,
            query_heads,
            query_patch,
            lax.all_gather(fresh_kv, "seq", axis=1, tiled=True),
            lax.all_gather(stale_own, "seq", axis=1, tiled=True),
            bounds,
        )
        blended = accumulated / denominator[:, :, None]
        return jnp.transpose(blended, (1, 0, 2)).reshape(tok_rows, head_cols).astype(jnp.bfloat16)

    def run_layer(incoming):
        features_all = lax.all_gather(incoming, "tp", axis=1, tiled=True).astype(jnp.float32)
        average = jnp.mean(features_all, axis=1, keepdims=True)
        centred = features_all - average
        variance = jnp.mean(centred * centred, axis=1, keepdims=True)
        normed = (centred * lax.rsqrt(variance + 1e-05) * (1.0 + scale_rows) + shift_rows).astype(
            jnp.bfloat16
        )
        proj = jnp.einsum("td,dcf->tcf", normed, weights_qkv, preferred_element_type=jnp.float32)
        queries = head_norm(proj[:, 0], gains[0])
        key_vecs = head_norm(proj[:, 1], gains[1])
        queries = jnp.where(
            video, queries * cosine + rotate_pairs(queries) * sine_table, queries
        ).astype(jnp.bfloat16)
        key_vecs = jnp.where(
            video, key_vecs * cosine + rotate_pairs(key_vecs) * sine_table, key_vecs
        ).astype(jnp.bfloat16)
        values = proj[:, 2].astype(jnp.bfloat16)
        fresh_kv = jnp.stack([key_vecs, values])
        attended = attend(queries, fresh_kv)
        projected = lax.psum_scatter(
            lax.dot_general(
                weights_out, attended, (((0,), (1,)), ((), ())), preferred_element_type=jnp.float32
            ).astype(jnp.bfloat16),
            "tp",
            scatter_dimension=0,
            tiled=True,
        ).astype(jnp.float32)
        result = (incoming.astype(jnp.float32) + gate_rows * projected.T).astype(jnp.bfloat16)
        return (result, fresh_kv)

    first_out, first_kv = run_layer(hidden)
    passed = shifted(first_out, "section", 1)
    second_out, second_kv = run_layer(passed)
    first_section = section_rank == 0
    hidden_out = jnp.where(first_section, first_out, second_out)[None]
    fresh_out = jnp.where(first_section, first_kv, second_kv)[None]
    return (hidden_out, fresh_out)


def solution(mesh):
    return jax.shard_map(
        local,
        mesh=mesh,
        in_specs=(
            P("seq", "tp"),
            P("section", None, None, "tp"),
            P("section", None, None),
            P("section", "tp", None),
            P("section", None, ("seq", "tp")),
            P("section", None, "seq", "tp"),
            P(),
            P(None, "seq"),
            P(),
        ),
        out_specs=(P("section", "seq", "tp"), P("section", None, "seq", "tp")),
        check_vma=False,
    )
```

profile of v0, /device:TPU:2, one launch (start us, length us, event | category | flops | bytes accessed | tf_op | source)
XLA Modules:
  0.0 375.8 jit_solution(1353841677514574803)
XLA Ops:
  8.2 1.3 dynamic-slice
  10.1 1.0 fusion.62
  11.3 10.7 %all-reduce.1 = f32[576]{0:T(1024)S(1)} all-reduce(f32[576]{0:T(1024)S(1)} %dynamic-update-slice), channel_id=2, replica_groups=mesh['section'=2,'seq'=32,'tp'=4] {'tp'}, use_global_device_ids=true, to_apply=%add.1 | all-reduce | flops 576 | bytes 4608
  22.1 42.5 %all_gather.23 = f32[32,8,144]{2,1,0:T(8,128)S(1)} all-gather(f32[1,8,144]{2,1,0:T(8,128)S(1)} %pad.4), channel_id=1, replica_groups=mesh['section'=2,'seq'=32,'tp'=4] {'seq'}, dimensions={0}, use_global_device_ids=true | all-gather | bytes 152064 | tf_op jit(solution)/shard_map/all_gather | solution.py:121
  64.9 12.3 %all_gather.24 = bf16[32,3072]{1,0:T(8,128)(2,1)S(1)} all-gather(bf16[32,768]{1,0:T(8,128)(2,1)} %param.9), channel_id=1, replica_groups=mesh['section'=2,'seq'=32,'tp'=4] {'tp'}, dimensions={1}, use_global_device_ids=true | all-gather | bytes 245760 | tf_op jit(solution)/shard_map/all_gather | solution.py:157
  77.6 4.4 %fusion.2 = f32[32,3,384]{2,0,1:T(8,128)S(1)} fusion(bf16[1,3072,3,384]{3,1,2,0:T(8,128)(2,1)} %param.10, bf16[32,3072]{1,0:T(8,128)(2,1)S(1)} %all_gather.24, f32[3072]{0:T(1024)S(1)} %bitcast.178, f32[3072]{0:T(1024)S(1)} %bitcast.180, f32[3072]{0:T(1024)S(1)} %bitcast.182, f32[3072]{0:T(1024)S(1)} %bitcast.176, f32[32]{0:T(128)S(1)} %add_rsqrt_fusion.5, ...), kind=kOutput, calls=%fused_computation.2 | convolution fusion | flops 227377152 | bytes 7471392 | tf_op jit(solution)/shard_map/td,dcf->tcf/dot_general | solution.py:164
  86.4 0.7 all-gather.10.cloned.1.call-update
  88.5 48.2 %all-gather.6.cloned.1.call-done = bf16[2,1024,384]{2,1,0:T(8,128)(2,1)} async-done(((bf16[2,32,384]{2,1,0:T(8,128)(2,1)}), bf16[2,1024,384]{2,1,0:T(8,128)(2,1)}) %all-gather.6.cloned.1.call-update) | async-done | bytes 1572880 | tf_op jit(solution)/shard_map/all_gather | solution.py:149
  136.7 2.4 fusion.128
  139.1 1.2 copy.165
  140.3 49.3 %all-gather.10.cloned.1.call-done = bf16[1,2,1024,384]{3,2,1,0:T(8,128)(2,1)} async-done(((bf16[1,2,32,384]{3,2,1,0:T(8,128)(2,1)}), bf16[1,2,1024,384]{3,2,1,0:T(8,128)(2,1)}) %all-gather.10.cloned.1.call-update) | async-done | bytes 1572880 | tf_op jit(solution)/shard_map/all_gather | solution.py:150
  189.6 2.7 fusion.127
  192.3 1.4 copy.166
  193.7 1.4 fusion.138
  195.1 1.1 fusion.136
  196.3 2.3 copy.167
  198.6 1.4 fusion.16
  200.0 2.4 fusion.28
  202.4 2.3 copy.168
  204.7 1.8 fusion.15
  206.6 1.2 fusion.4
  208.0 21.3 %reduce-scatter.3.cloned.1.call-done = bf16[768,32]{0,1:T(8,128)(2,1)} async-done(((bf16[3072,32]{0,1:T(8,128)(2,1)}), bf16[768,32]{0,1:T(8,128)(2,1)}) %reduce-scatter.3.cloned.1.call-update) | async-done | bytes 49168 | tf_op jit(solution)/shard_map/reduce_scatter | solution.py:176
  229.3 0.9 fusion.65
  230.2 3.5 collective-permute-start
  233.6 1.7 collective-permute-done
  236.0 12.1 %all_gather.27 = bf16[32,3072]{1,0:T(8,128)(2,1)S(1)} all-gather(bf16[32,768]{1,0:T(8,128)(2,1)S(1)} %collective-permute-done), channel_id=1, replica_groups=mesh['section'=2,'seq'=32,'tp'=4] {'tp'}, dimensions={1}, use_global_device_ids=true | all-gather | bytes 245760 | tf_op jit(solution)/shard_map/all_gather | solution.py:157
  248.5 4.4 %fusion = f32[32,3,384]{2,0,1:T(8,128)S(1)} fusion(bf16[1,3072,3,384]{3,1,2,0:T(8,128)(2,1)} %param.10, bf16[32,3072]{1,0:T(8,128)(2,1)S(1)} %all_gather.27, f32[32]{0:T(128)S(1)} %add_rsqrt_fusion.4, f32[32]{0:T(128)S(1)} %broadcast_multiply_fusion.7, f32[3072]{0:T(1024)S(1)} %bitcast.179, f32[3072]{0:T(1024)S(1)} %bitcast.181, f32[3072]{0:T(1024)S(1)} %bitcast.183, ...), kind=kOutput, calls=%fused_computation | convolution fusion | flops 227377152 | bytes 7471392 | tf_op jit(solution)/shard_map/td,dcf->tcf/dot_general | solution.py:164
  254.5 0.7 mul.489
  255.2 0.9 reshape_squeeze.53
  256.1 0.7 reduce_sum.159
  256.8 1.3 broadcast_multiply_fusion.1
  258.1 1.4 copy.170
  259.5 1.4 multiply_reduce_fusion.2
  260.9 1.4 copy.172
  262.3 0.7 add_rsqrt_fusion.1
  263.6 0.8 mul.475.clone
  264.4 1.6 mul.479
  266.0 1.5 sub.161.clone
  267.4 1.6 sub.163
  269.0 1.5 sub.165
  270.5 1.6 sub.169
  272.1 1.5 fusion.93
  273.6 0.7 slice_bitcast_fusion
  274.3 0.7 slice_bitcast_fusion.4
  275.0 0.7 mul.485
  275.7 1.0 sub.166
  277.3 1.0 fusion.87
  279.8 0.8 copy.173
  280.6 0.8 fusion.133
  281.4 1.0 fusion.132
  282.5 0.7 pad_maximum_fusion.2
  283.2 0.9 concatenate.137
  284.1 1.5 fusion.71
  285.6 45.9 %all-gather.8.cloned.1.call-done = bf16[2,1024,384]{2,1,0:T(8,128)(2,1)} async-done(((bf16[2,32,384]{2,1,0:T(8,128)(2,1)}), bf16[2,1024,384]{2,1,0:T(8,128)(2,1)}) %all-gather.8.cloned.1.call-update) | async-done | bytes 1572880 | tf_op jit(solution)/shard_map/all_gather | solution.py:149
  331.5 2.6 fusion.126
  334.2 2.3 copy.180
  336.5 1.4 fusion.139
  337.9 1.2 fusion.137
  339.0 2.4 copy.181
  341.4 1.5 fusion.17
  342.9 1.5 fusion.29
  345.1 1.2 fusion.5
  347.0 20.8 %reduce-scatter.5.cloned.1.call-done = bf16[768,32]{0,1:T(8,128)(2,1)} async-done(((bf16[3072,32]{0,1:T(8,128)(2,1)}), bf16[768,32]{0,1:T(8,128)(2,1)}) %reduce-scatter.5.cloned.1.call-update) | async-done | bytes 49168 | tf_op jit(solution)/shard_map/reduce_scatter | solution.py:176
  367.8 1.5 fusion.77
  (190 shorter events, 13.3 us)
Async XLA Ops:
  7.2 199.4 %copy-start = (bf16[1,384,3072]{2,1,0:T(8,128)(2,1)S(1)}, bf16[1,384,3072]{2,1,0:T(8,128)(2,1)}, u32[]{:S(2)}) copy-start(bf16[1,384,3072]{2,1,0:T(8,128)(2,1)} %param.12) | copy-start | bytes 7077892
  7.2 129.5 %all-gather.6.cloned.1.call-start = ((), (), s32[]{:S(2)}) async-start(), calls=%async_computation.2 | async-start | bytes 1622016 | tf_op jit(solution)/shard_map/all_gather | solution.py:149
  7.3 241.3 %copy-start.28 = (pred[32]{0:T(512)(128)(4,1)}, pred[32]{0:T(512)(128)(4,1)S(1)}, u32[]{:S(2)}) copy-start(pred[32]{0:T(512)(128)(4,1)S(1)} %fusion.119) | copy-start | bytes 100
  82.0 1.8 copy-start.35
  82.1 2.9 copy-start.34
  83.1 4.7 %copy-start.36 = (s32[4]{0:T(128)S(1)}, s32[4]{0:T(128)}, u32[]{:S(2)}) copy-start(s32[4]{0:T(128)} %param.15) | copy-start | bytes 52
  83.8 55.3 %copy-start.31 = (f32[64]{0:T(128)}, f32[64]{0:T(128)S(1)}, u32[]{:S(2)}) copy-start(f32[64]{0:T(128)S(1)} %get-tuple-element.47) | copy-start | bytes 772
  83.9 4.3 %copy-start.30 = (f32[384]{0:T(512)}, f32[384]{0:T(512)S(1)}, u32[]{:S(2)}) copy-start(f32[384]{0:T(512)S(1)} %mul.449) | copy-start | bytes 4612
  84.0 4.2 %copy-start.23 = (f32[384]{0:T(512)}, f32[384]{0:T(512)S(1)}, u32[]{:S(2)}) copy-start(f32[384]{0:T(512)S(1)} %mul.459) | copy-start | bytes 4612
  84.4 54.8 %copy-start.33 = (pred[384]{0:T(512)(128)(4,1)}, pred[384]{0:T(512)(128)(4,1)S(1)}, u32[]{:S(2)}) copy-start(pred[384]{0:T(512)(128)(4,1)S(1)} %fusion.111) | copy-start | bytes 1156
  85.3 3.1 copy-start.8
  85.4 3.1 copy-start.9
  85.5 3.0 copy-start.6
  85.6 2.9 copy-start.7
  85.7 1.9 copy-start.10
  86.4 103.3 %all-gather.10.cloned.1.call-start = ((), (), s32[]{:S(2)}) async-start(), calls=%async_computation.6 | async-start | bytes 1622016 | tf_op jit(solution)/shard_map/all_gather | solution.py:150
  87.1 142.1 %reduce-scatter.3.cloned.1.call-start = ((), (), s32[]{:S(2)}) async-start(), calls=%async_computation.3 | async-start | bytes 245760 | tf_op jit(solution)/shard_map/reduce_scatter | solution.py:176
  88.0 0.5 copy-start.32
  88.3 116.4 %copy-start.2 = (pred[32,1024]{1,0:T(8,128)(4,1)}, pred[32,1024]{1,0:T(8,128)(4,1)S(1)}, u32[]{:S(2)}) copy-start(pred[32,1024]{1,0:T(8,128)(4,1)S(1)} %broadcast_compare_fusion) | copy-start | bytes 98308
  204.7 24.6 %copy-start.16 = (bf16[32,768]{1,0:T(8,128)(2,1)S(1)}, bf16[32,768]{1,0:T(8,128)(2,1)}, u32[]{:S(2)}) copy-start(bf16[32,768]{1,0:T(8,128)(2,1)} %param.9) | copy-start | bytes 147460
  207.8 123.7 %all-gather.8.cloned.1.call-start = ((), (), s32[]{:S(2)}) async-start(), calls=%async_computation.4 | async-start | bytes 1622016 | tf_op jit(solution)/shard_map/all_gather | solution.py:149
  208.0 40.5 %copy-start.24 = (f32[768]{0:T(1024)}, f32[768]{0:T(1024)S(1)}, u32[]{:S(2)}) copy-start(f32[768]{0:T(1024)S(1)} %get-tuple-element.2) | copy-start | bytes 9220
  208.0 40.5 %copy-start.26 = (f32[768]{0:T(1024)}, f32[768]{0:T(1024)S(1)}, u32[]{:S(2)}) copy-start(f32[768]{0:T(1024)S(1)} %get-tuple-element.3) | copy-start | bytes 9220
  230.2 18.4 %copy-start.14 = (bf16[32,768]{1,0:T(8,128)(2,1)}, bf16[32,768]{1,0:T(8,128)(2,1)S(1)}, u32[]{:S(2)}) copy-start(bf16[32,768]{1,0:T(8,128)(2,1)S(1)} %fusion.65) | copy-start | bytes 147460
  230.2 5.2 %collective-permute-start = (bf16[32,768]{1,0:T(8,128)(2,1)S(1)}, bf16[32,768]{1,0:T(8,128)(2,1)S(1)}, u32[]{:S(2)}, u32[]{:S(2)}) collective-permute-start(bf16[32,768]{1,0:T(8,128)(2,1)S(1)} %fusion.65), channel_id=1, source_target_pairs={{0,128},{1,129},{2,130},{3,131},{4,132},{5,133},{6,134},{7,135},{8... | collective-permute-start | bytes 147464 | tf_op jit(solution)/shard_map/ppermute | solution.py:15
  235.4 0.6 copy-start.17
  253.8 0.6 copy-start.19
  263.0 0.6 copy-start.20
  278.3 0.6 copy-start.12
  279.6 88.2 %reduce-scatter.5.cloned.1.call-start = ((), (), s32[]{:S(2)}) async-start(), calls=%async_computation.5 | async-start | bytes 245760 | tf_op jit(solution)/shard_map/reduce_scatter | solution.py:176
  285.6 50.9 %copy-start.5 = (bf16[32,6,64]{2,0,1:T(8,128)(2,1)S(1)}, bf16[32,6,64]{2,0,1:T(8,128)(2,1)}, u32[]{:S(2)}) copy-start(bf16[32,6,64]{2,0,1:T(8,128)(2,1)} %fusion.71) | copy-start | bytes 73732
  334.2 3.7 copy-start.3
  339.0 3.8 %copy-start.1 = (f32[6,32,1024]{2,1,0:T(8,128)S(1)}, f32[6,32,1024]{2,1,0:T(8,128)}, u32[]{:S(2)}) copy-start(f32[6,32,1024]{2,1,0:T(8,128)} %get-tuple-element.54) | copy-start | bytes 2359300
  341.4 3.0 copy-start.4
  344.4 1.9 copy-start.11
  344.4 1.9 copy-start.13
  344.4 1.9 copy-start.21
  344.5 1.9 copy-start.22
  344.5 23.3 %copy-start.15 = (bf16[32,768]{1,0:T(8,128)(2,1)S(1)}, bf16[32,768]{1,0:T(8,128)(2,1)}, u32[]{:S(2)}) copy-start(bf16[32,768]{1,0:T(8,128)(2,1)} %copy-done.14) | copy-start | bytes 147460
  344.5 23.3 %copy-start.18 = (bf16[32,768]{1,0:T(8,128)(2,1)S(1)}, bf16[32,768]{1,0:T(8,128)(2,1)}, u32[]{:S(2)}) copy-start(bf16[32,768]{1,0:T(8,128)(2,1)} %copy-done.17) | copy-start | bytes 147460
  344.5 23.3 %copy-start.25 = (f32[768]{0:T(1024)S(1)}, f32[768]{0:T(1024)}, u32[]{:S(2)}) copy-start(f32[768]{0:T(1024)} %copy-done.24) | copy-start | bytes 9220
  344.5 23.3 %copy-start.27 = (f32[768]{0:T(1024)S(1)}, f32[768]{0:T(1024)}, u32[]{:S(2)}) copy-start(f32[768]{0:T(1024)} %copy-done.26) | copy-start | bytes 9220
  344.5 23.3 %copy-start.29 = (pred[32]{0:T(512)(128)(4,1)S(1)}, pred[32]{0:T(512)(128)(4,1)}, u32[]{:S(2)}) copy-start(pred[32]{0:T(512)(128)(4,1)} %copy-done.28) | copy-start | bytes 100
Sparse Core Ops, SparseCore 0:
  86.5 50.1 all-gather.5
  139.3 50.2 all-gather.9
  208.0 21.2 reduce-scatter.2
  279.7 51.7 all-gather.7
  346.4 21.3 reduce-scatter.4
where the time goes:
time: 378 us; the launch traced here: 376 us
  waiting for transfers between devices  188 us (50%)
  blocking collectives  77.7 us (21%)
  local copies, waits for them, and re-layouts  47.8 us (13%)
  matrix products  23.4 us (6%)
  other arithmetic  19 us (5%)
  between operations  16.1 us (4%)
  starting transfers between devices  3.86 us (1%)
    all_gather x2, waiting for transfers between devices, attend(): lax.all_gather(fresh_kv, 'seq', axis=1, tiled=True)  94.1 us
    all_gather x1, waiting for transfers between devices, attend(): lax.all_gather(stale_own, 'seq', axis=1, tiled=True)  49.3 us
    all_gather x1, blocking collectives, local(): lax.all_gather(jnp.pad(by_tp.reshape(1, 4, -1), ((0, 0), (0, 4), (0, 0)))...  42.5 us
    reduce_scatter x2, waiting for transfers between devices, run_layer(): lax.psum_scatter(lax.dot_general(weights_out, attended, (((0,), (1,)), ((...  42 us
    all_gather x2, blocking collectives, run_layer(): lax.all_gather(incoming, 'tp', axis=1, tiled=True).astype(jnp.float32)  24.5 us
    unnamed x1, blocking collectives  10.7 us
    dot_general x2, matrix products, run_layer(): jnp.einsum('td,dcf->tcf', normed, weights_qkv, preferred_element_type=jnp...  8.79 us
    slice x4, local copies, waits for them, and re-layouts, merge_block(): fresh_keys = fresh_block[0].reshape(key_count, head_count, HEAD)  8.52 us
  transfers between devices with their start and end apart: 6, of which 6 were waited for; matrix products, arithmetic and copies ran while one was open for 3% of the time, Pallas kernels for 0%

commit v1 on v0

--- a/solution.py
+++ b/solution.py
@@ -154,7 +154,9 @@
         return jnp.transpose(blended, (1, 0, 2)).reshape(tok_rows, head_cols).astype(jnp.bfloat16)
 
     def run_layer(incoming):
-        features_all = lax.all_gather(incoming, "tp", axis=1, tiled=True).astype(jnp.float32)
+        features_all = jnp.concatenate(
+            lax.all_to_all(jnp.stack([incoming] * lax.axis_size("tp")), "tp", 0, 0), axis=1
+        ).astype(jnp.float32)
         average = jnp.mean(features_all, axis=1, keepdims=True)
         centred = features_all - average
         variance = jnp.mean(centred * centred, axis=1, keepdims=True)

time: 378 us -> 314 us (0.83)
  waiting for transfers between devices: 188 us -> 131 us
  blocking collectives: 77.7 us -> 62.8 us
  local copies, waits for them, and re-layouts: 47.8 us -> 52.3 us
  starting transfers between devices: 3.86 us -> 8.28 us
    all_gather x1, waiting for transfers between devices: 49.3 us -> 0.02 us  [attend(): lax.all_gather(stale_own, 'seq', axis=1, tiled=True)]
    all_gather x2 -> x0, blocking collectives: 24.5 us -> none  [run_layer(): lax.all_gather(incoming, 'tp', axis=1, tiled=True).astype(jnp.float32)]
    all_to_all x0 -> x1, blocking collectives: none -> 8.88 us  [run_layer(): lax.all_to_all(jnp.stack([incoming] * lax.axis_size('tp')), 'tp', 0, 0)]
    all_gather x2, waiting for transfers between devices: 94.1 us -> 86.8 us  [attend(): lax.all_gather(fresh_kv, 'seq', axis=1, tiled=True)]
    all_to_all x0 -> x1, starting transfers between devices: none -> 4.46 us  [run_layer(): lax.all_to_all(jnp.stack([incoming] * lax.axis_size('tp')), 'tp', 0, 0)]
  transfers between devices with their start and end apart: 6 -> 7, of which waited for: 6 -> 5; matrix products, arithmetic and copies ran while one was open for 3% -> 9% of each run, Pallas kernels for 0% -> 0%
where the time goes in v1:
time: 314 us; the launch traced here: 312 us
  waiting for transfers between devices  131 us (42%)
  blocking collectives  62.8 us (20%)
  local copies, waits for them, and re-layouts  52.3 us (17%)
  matrix products  21.1 us (7%)
  other arithmetic  20.2 us (6%)
  between operations  16 us (5%)
  starting transfers between devices  8.28 us (3%)
    all_gather x2, waiting for transfers between devices, attend(): lax.all_gather(fresh_kv, 'seq', axis=1, tiled=True)  86.8 us
    all_gather x1, blocking collectives, local(): lax.all_gather(jnp.pad(by_tp.reshape(1, 4, -1), ((0, 0), (0, 4), (0, 0)))...  43 us
    reduce_scatter x2, waiting for transfers between devices, run_layer(): lax.psum_scatter(lax.dot_general(weights_out, attended, (((0,), (1,)), ((...  42.1 us
    unnamed x1, blocking collectives  10.9 us
    slice x4, local copies, waits for them, and re-layouts, merge_block(): fresh_keys = fresh_block[0].reshape(key_count, head_count, HEAD)  10 us
    all_to_all x1, blocking collectives, run_layer(): lax.all_to_all(jnp.stack([incoming] * lax.axis_size('tp')), 'tp', 0, 0)  8.88 us
    dot_general x2, matrix products, run_layer(): jnp.einsum('td,dcf->tcf', normed, weights_qkv, preferred_element_type=jnp...  8.5 us
    sub x10, local copies, waits for them, and re-layouts, head_norm(): centred = parts - average  7.52 us
  transfers between devices with their start and end apart: 7, of which 5 were waited for; matrix products, arithmetic and copies ran while one was open for 9% of the time, Pallas kernels for 0%

profile of v1, /device:TPU:2, one launch (start us, length us, event | category | flops | bytes accessed | tf_op | source)
XLA Modules:
  0.0 312.1 jit_solution(17483355378526559876)
XLA Ops:
  7.2 1.6 stack.36
  8.8 4.5 %all-to-all-start = ((bf16[4,32,768]{2,1,0:T(8,128)(2,1)}), bf16[4,32,768]{2,1,0:T(8,128)(2,1)S(1)}, u32[]{:S(2)}, u32[]{:S(2)}) async-start(bf16[4,32,768]{2,1,0:T(8,128)(2,1)} %stack.36), calls=%async_computation | async-start | bytes 393216 | tf_op jit(solution)/shard_map/all_to_all | solution.py:158
  13.3 0.7 all-gather.10.cloned.1.call-update
  14.8 1.3 dynamic-slice
  16.7 1.0 fusion.44
  18.0 10.9 %all-reduce.1 = f32[576]{0:T(1024)S(1)} all-reduce(f32[576]{0:T(1024)S(1)} %dynamic-update-slice), channel_id=2, replica_groups=mesh['section'=2,'seq'=32,'tp'=4] {'tp'}, use_global_device_ids=true, to_apply=%add.1 | all-reduce | flops 576 | bytes 4608
  29.0 43.0 %all_gather.17 = f32[32,8,144]{2,1,0:T(8,128)S(1)} all-gather(f32[1,8,144]{2,1,0:T(8,128)S(1)} %pad.4), channel_id=1, replica_groups=mesh['section'=2,'seq'=32,'tp'=4] {'seq'}, dimensions={0}, use_global_device_ids=true | all-gather | bytes 152064 | tf_op jit(solution)/shard_map/all_gather | solution.py:121
  72.3 0.8 slice_bitcast_fusion.12
  73.1 0.7 convert_element_type.206
  75.6 4.3 %fusion.2 = f32[32,3,384]{2,0,1:T(8,128)S(1)} fusion(bf16[32,3072,1]{1,0,2:T(8,128)(2,1)S(1)} %reshape.1119, bf16[1,3072,3,384]{3,1,2,0:T(8,128)(2,1)} %param.10), kind=kOutput, calls=%fused_computation.2 | convolution fusion | flops 226492416 | bytes 7421952 | tf_op jit(solution)/shard_map/td,dcf->tcf/dot_general | solution.py:166
  84.7 2.7 fusion.107
  87.4 1.4 copy.193
  88.8 2.3 copy.195
  91.1 41.8 %all-gather.6.cloned.1.call-done = bf16[2,1024,384]{2,1,0:T(8,128)(2,1)} async-done(((bf16[2,32,384]{2,1,0:T(8,128)(2,1)}), bf16[2,1024,384]{2,1,0:T(8,128)(2,1)}) %all-gather.6.cloned.1.call-update) | async-done | bytes 1572880 | tf_op jit(solution)/shard_map/all_gather | solution.py:149
  132.9 2.7 fusion.108
  135.6 2.3 copy.192
  137.9 1.4 fusion.117
  139.3 1.2 fusion.115
  140.4 2.3 copy.194
  142.7 1.5 fusion.16
  144.2 1.8 fusion.30
  146.6 1.2 fusion.4
  148.0 21.3 %reduce-scatter.3.cloned.1.call-done = bf16[768,32]{0,1:T(8,128)(2,1)} async-done(((bf16[3072,32]{0,1:T(8,128)(2,1)}), bf16[768,32]{0,1:T(8,128)(2,1)}) %reduce-scatter.3.cloned.1.call-update) | async-done | bytes 49168 | tf_op jit(solution)/shard_map/reduce_scatter | solution.py:178
  169.3 0.9 fusion.47
  170.2 3.5 %collective-permute-start = (bf16[32,768]{1,0:T(8,128)(2,1)S(1)}, bf16[32,768]{1,0:T(8,128)(2,1)S(1)}, u32[]{:S(2)}, u32[]{:S(2)}) collective-permute-start(bf16[32,768]{1,0:T(8,128)(2,1)S(1)} %fusion.47), channel_id=1, source_target_pairs={{0,128},{1,129},{2,130},{3,131},{4,132},{5,133},{6,134},{7,135},{8... | collective-permute-start | bytes 147464 | tf_op jit(solution)/shard_map/ppermute | solution.py:15
  173.7 1.7 collective-permute-done
  175.4 8.9 %all_to_all.10 = bf16[4,32,768]{2,1,0:T(8,128)(2,1)S(1)} all-to-all(bf16[4,32,768]{2,1,0:T(8,128)(2,1)S(1)} %stack.38), channel_id=1, replica_groups=mesh['section'=2,'seq'=32,'tp'=4] {'tp'}, dimensions={0} | all-to-all | bytes 393216 | tf_op jit(solution)/shard_map/all_to_all | solution.py:158
  185.2 4.3 %fusion = f32[32,3,384]{2,0,1:T(8,128)S(1)} fusion(bf16[32,3072,1]{1,0,2:T(8,128)(2,1)S(1)} %reshape.1120, bf16[1,3072,3,384]{3,1,2,0:T(8,128)(2,1)} %param.10), kind=kOutput, calls=%fused_computation | convolution fusion | flops 226492416 | bytes 7421952 | tf_op jit(solution)/shard_map/td,dcf->tcf/dot_general | solution.py:166
  191.0 0.7 mul.505
  191.7 0.9 reshape_squeeze.53
  192.6 0.7 reduce_sum.159
  193.3 1.3 broadcast_multiply_fusion.1
  194.6 1.4 copy.198
  196.0 1.4 multiply_reduce_fusion.2
  197.5 1.4 copy.200
  198.8 0.7 add_rsqrt_fusion.1
  200.2 0.7 mul.491.clone
  200.9 1.6 mul.495
  202.5 1.5 sub.167.clone
  204.0 1.6 sub.169
  205.6 1.5 sub.171
  207.0 1.6 sub.175
  208.6 1.5 fusion.75
  210.1 0.7 slice_bitcast_fusion
  211.5 0.7 mul.501
  212.2 1.0 sub.172
  213.8 1.0 fusion.69
  216.3 1.4 copy.201
  217.7 0.8 fusion.112
  218.5 1.0 fusion.111
  219.6 0.7 pad_maximum_fusion.2
  220.3 0.9 concatenate.137
  221.2 1.5 fusion.53
  222.7 45.0 %all-gather.8.cloned.1.call-done = bf16[2,1024,384]{2,1,0:T(8,128)(2,1)} async-done(((bf16[2,32,384]{2,1,0:T(8,128)(2,1)}), bf16[2,1024,384]{2,1,0:T(8,128)(2,1)}) %all-gather.8.cloned.1.call-update) | async-done | bytes 1572880 | tf_op jit(solution)/shard_map/all_gather | solution.py:149
  267.7 2.7 fusion.106
  270.4 2.3 copy.208
  272.7 1.4 fusion.118
  274.1 1.1 fusion.116
  275.3 2.4 copy.209
  277.6 1.5 fusion.17
  279.1 1.5 fusion.31
  281.3 1.2 fusion.5
  283.2 20.8 %reduce-scatter.5.cloned.1.call-done = bf16[768,32]{0,1:T(8,128)(2,1)} async-done(((bf16[3072,32]{0,1:T(8,128)(2,1)}), bf16[768,32]{0,1:T(8,128)(2,1)}) %reduce-scatter.5.cloned.1.call-update) | async-done | bytes 49168 | tf_op jit(solution)/shard_map/reduce_scatter | solution.py:178
  304.1 1.5 fusion.59
  (203 shorter events, 14.8 us)
Async XLA Ops:
  7.2 139.4 %copy-start = (bf16[1,384,3072]{2,1,0:T(8,128)(2,1)S(1)}, bf16[1,384,3072]{2,1,0:T(8,128)(2,1)}, u32[]{:S(2)}) copy-start(bf16[1,384,3072]{2,1,0:T(8,128)(2,1)} %param.12) | copy-start | bytes 7077892
  8.8 65.9 %all-to-all-start = ((bf16[4,32,768]{2,1,0:T(8,128)(2,1)}), bf16[4,32,768]{2,1,0:T(8,128)(2,1)S(1)}, u32[]{:S(2)}, u32[]{:S(2)}) async-start(bf16[4,32,768]{2,1,0:T(8,128)(2,1)} %stack.36), calls=%async_computation | async-start | bytes 393216 | tf_op jit(solution)/shard_map/all_to_all | solution.py:158
  13.3 71.4 %all-gather.10.cloned.1.call-start = ((), (), s32[]{:S(2)}) async-start(), calls=%async_computation.8 | async-start | bytes 1622016 | tf_op jit(solution)/shard_map/all_gather | solution.py:150
  14.0 118.9 %all-gather.6.cloned.1.call-start = ((), (), s32[]{:S(2)}) async-start(), calls=%async_computation.4 | async-start | bytes 1622016 | tf_op jit(solution)/shard_map/all_gather | solution.py:149
  73.1 11.4 %copy-start.33 = (f32[64]{0:T(128)}, f32[64]{0:T(128)S(1)}, u32[]{:S(2)}) copy-start(f32[64]{0:T(128)S(1)} %get-tuple-element.47) | copy-start | bytes 772
  74.0 8.5 %copy-start.35 = (pred[384]{0:T(512)(128)(4,1)}, pred[384]{0:T(512)(128)(4,1)S(1)}, u32[]{:S(2)}) copy-start(pred[384]{0:T(512)(128)(4,1)S(1)} %fusion.93) | copy-start | bytes 1156
  74.2 7.6 %copy-start.32 = (f32[384]{0:T(512)}, f32[384]{0:T(512)S(1)}, u32[]{:S(2)}) copy-start(f32[384]{0:T(512)S(1)} %mul.464) | copy-start | bytes 4612
  74.3 8.3 %copy-start.25 = (f32[384]{0:T(512)}, f32[384]{0:T(512)S(1)}, u32[]{:S(2)}) copy-start(f32[384]{0:T(512)S(1)} %mul.474) | copy-start | bytes 4612
  74.3 10.2 %copy-start.10 = (f32[32,64]{1,0:T(8,128)}, f32[32,64]{1,0:T(8,128)S(1)}, u32[]{:S(2)}) copy-start(f32[32,64]{1,0:T(8,128)S(1)} %copy.182) | copy-start | bytes 24580
  74.4 10.1 %copy-start.11 = (f32[32,64]{1,0:T(8,128)}, f32[32,64]{1,0:T(8,128)S(1)}, u32[]{:S(2)}) copy-start(f32[32,64]{1,0:T(8,128)S(1)} %copy.187) | copy-start | bytes 24580
  74.6 8.0 %copy-start.8 = (f32[1,32,384]{2,1,0:T(8,128)}, f32[1,32,384]{2,1,0:T(8,128)S(1)}, u32[]{:S(2)}) copy-start(f32[1,32,384]{2,1,0:T(8,128)S(1)} %tile.20) | copy-start | bytes 147460
  74.6 7.9 %copy-start.9 = (f32[1,32,384]{2,1,0:T(8,128)}, f32[1,32,384]{2,1,0:T(8,128)S(1)}, u32[]{:S(2)}) copy-start(f32[1,32,384]{2,1,0:T(8,128)S(1)} %tile.21) | copy-start | bytes 147460
  74.7 110.0 %copy-start.30 = (pred[32]{0:T(512)(128)(4,1)}, pred[32]{0:T(512)(128)(4,1)S(1)}, u32[]{:S(2)}) copy-start(pred[32]{0:T(512)(128)(4,1)S(1)} %fusion.101) | copy-start | bytes 100
  79.8 3.6 %copy-start.36 = (s32[4]{0:T(128)S(1)}, s32[4]{0:T(128)}, u32[]{:S(2)}) copy-start(s32[4]{0:T(128)} %param.15) | copy-start | bytes 52
  82.7 1.7 copy-start.12
  83.3 86.0 %reduce-scatter.3.cloned.1.call-start = ((), (), s32[]{:S(2)}) async-start(), calls=%async_computation.5 | async-start | bytes 245760 | tf_op jit(solution)/shard_map/reduce_scatter | solution.py:178
  83.6 5.2 %copy-start.34 = (pred[6,64]{1,0:T(8,128)(4,1)}, pred[6,64]{1,0:T(8,128)(4,1)S(1)}, u32[]{:S(2)}) copy-start(pred[6,64]{1,0:T(8,128)(4,1)S(1)} %fusion.88) | copy-start | bytes 1156
  83.9 62.1 %copy-start.3 = (pred[32,1024]{1,0:T(8,128)(4,1)}, pred[32,1024]{1,0:T(8,128)(4,1)S(1)}, u32[]{:S(2)}) copy-start(pred[32,1024]{1,0:T(8,128)(4,1)S(1)} %broadcast_compare_fusion) | copy-start | bytes 98308
  142.7 3.3 %copy-start.2 = (f32[6,32,1024]{2,1,0:T(8,128)S(1)}, f32[6,32,1024]{2,1,0:T(8,128)}, u32[]{:S(2)}) copy-start(f32[6,32,1024]{2,1,0:T(8,128)} %get-tuple-element.52) | copy-start | bytes 2359300
  142.7 3.3 %copy-start.5 = (bf16[1,1,1024,384]{2,3,1,0:T(8,128)(2,1)S(1)}, bf16[1,1,1024,384]{2,3,1,0:T(8,128)(2,1)}, u32[]{:S(2)}) copy-start(bf16[1,1,1024,384]{2,3,1,0:T(8,128)(2,1)} %copy.195) | copy-start | bytes 2359300
  146.0 23.3 %copy-start.18 = (bf16[32,768]{1,0:T(8,128)(2,1)S(1)}, bf16[32,768]{1,0:T(8,128)(2,1)}, u32[]{:S(2)}) copy-start(bf16[32,768]{1,0:T(8,128)(2,1)} %param.9) | copy-start | bytes 147460
  147.8 119.9 %all-gather.8.cloned.1.call-start = ((), (), s32[]{:S(2)}) async-start(), calls=%async_computation.6 | async-start | bytes 1622016 | tf_op jit(solution)/shard_map/all_gather | solution.py:149
  148.0 36.7 %copy-start.26 = (f32[768]{0:T(1024)}, f32[768]{0:T(1024)S(1)}, u32[]{:S(2)}) copy-start(f32[768]{0:T(1024)S(1)} %get-tuple-element.2) | copy-start | bytes 9220
  148.0 36.7 %copy-start.28 = (f32[768]{0:T(1024)}, f32[768]{0:T(1024)S(1)}, u32[]{:S(2)}) copy-start(f32[768]{0:T(1024)S(1)} %get-tuple-element.3) | copy-start | bytes 9220
  170.2 3.5 %copy-start.16 = (bf16[32,768]{1,0:T(8,128)(2,1)}, bf16[32,768]{1,0:T(8,128)(2,1)S(1)}, u32[]{:S(2)}) copy-start(bf16[32,768]{1,0:T(8,128)(2,1)S(1)} %fusion.47) | copy-start | bytes 147460
  170.2 5.2 %collective-permute-start = (bf16[32,768]{1,0:T(8,128)(2,1)S(1)}, bf16[32,768]{1,0:T(8,128)(2,1)S(1)}, u32[]{:S(2)}, u32[]{:S(2)}) collective-permute-start(bf16[32,768]{1,0:T(8,128)(2,1)S(1)} %fusion.47), channel_id=1, source_target_pairs={{0,128},{1,129},{2,130},{3,131},{4,132},{5,133},{6,134},{7,135},{8... | collective-permute-start | bytes 147464 | tf_op jit(solution)/shard_map/ppermute | solution.py:15
  175.4 9.3 %copy-start.19 = (bf16[32,768]{1,0:T(8,128)(2,1)}, bf16[32,768]{1,0:T(8,128)(2,1)S(1)}, u32[]{:S(2)}) copy-start(bf16[32,768]{1,0:T(8,128)(2,1)S(1)} %collective-permute-done) | copy-start | bytes 147460
  190.3 0.6 copy-start.21
  199.6 0.6 copy-start.22
  214.8 0.6 copy-start.14
  216.1 88.0 %reduce-scatter.5.cloned.1.call-start = ((), (), s32[]{:S(2)}) async-start(), calls=%async_computation.7 | async-start | bytes 245760 | tf_op jit(solution)/shard_map/reduce_scatter | solution.py:178
  222.7 50.0 %copy-start.7 = (bf16[32,6,64]{2,0,1:T(8,128)(2,1)S(1)}, bf16[32,6,64]{2,0,1:T(8,128)(2,1)}, u32[]{:S(2)}) copy-start(bf16[32,6,64]{2,0,1:T(8,128)(2,1)} %fusion.53) | copy-start | bytes 73732
  270.4 3.7 %copy-start.4 = (pred[32,1024]{1,0:T(8,128)(4,1)S(1)}, pred[32,1024]{1,0:T(8,128)(4,1)}, u32[]{:S(2)}) copy-start(pred[32,1024]{1,0:T(8,128)(4,1)} %copy-done.3) | copy-start | bytes 98308
  275.3 3.8 %copy-start.1 = (f32[6,32,1024]{2,1,0:T(8,128)S(1)}, f32[6,32,1024]{2,1,0:T(8,128)}, u32[]{:S(2)}) copy-start(f32[6,32,1024]{2,1,0:T(8,128)} %get-tuple-element.54) | copy-start | bytes 2359300
  277.6 3.0 copy-start.6
  280.7 1.9 copy-start.13
  280.7 1.9 copy-start.15
  280.7 1.9 copy-start.23
  280.7 1.9 copy-start.24
  280.7 23.3 %copy-start.17 = (bf16[32,768]{1,0:T(8,128)(2,1)S(1)}, bf16[32,768]{1,0:T(8,128)(2,1)}, u32[]{:S(2)}) copy-start(bf16[32,768]{1,0:T(8,128)(2,1)} %copy-done.16) | copy-start | bytes 147460
  280.7 23.3 %copy-start.20 = (bf16[32,768]{1,0:T(8,128)(2,1)S(1)}, bf16[32,768]{1,0:T(8,128)(2,1)}, u32[]{:S(2)}) copy-start(bf16[32,768]{1,0:T(8,128)(2,1)} %copy-done.19) | copy-start | bytes 147460
  280.7 23.3 %copy-start.27 = (f32[768]{0:T(1024)S(1)}, f32[768]{0:T(1024)}, u32[]{:S(2)}) copy-start(f32[768]{0:T(1024)} %copy-done.26) | copy-start | bytes 9220
  280.7 23.3 %copy-start.29 = (f32[768]{0:T(1024)S(1)}, f32[768]{0:T(1024)}, u32[]{:S(2)}) copy-start(f32[768]{0:T(1024)} %copy-done.28) | copy-start | bytes 9220
  280.8 23.3 %copy-start.31 = (pred[32]{0:T(512)(128)(4,1)S(1)}, pred[32]{0:T(512)(128)(4,1)}, u32[]{:S(2)}) copy-start(pred[32]{0:T(512)(128)(4,1)} %copy-done.30) | copy-start | bytes 100
Sparse Core Ops, SparseCore 0:
  16.7 55.4 all-gather.9
  83.4 49.4 all-gather.5
  148.0 21.2 reduce-scatter.2
  216.2 51.4 all-gather.7
  282.7 21.3 reduce-scatter.4
